TPU v7x, 256 devices: a whole 4x4x8 slice. The times are simulated.
256 devices in a mesh: vec: 16 (over y, z_lo, core), state: 16 (over x, z_hi).
Axes of the slice: x: 4, y: 4, z: 8 (z_hi: 4, z_lo: 2; z = z_hi * 2 + z_lo), core: 2. Of those that a mesh axis runs over, the one named last changes fastest.
Arguments:
- beliefs: bfloat16 [2048, 32768], P('vec', 'state'), may hold values from 0.05 to 1
- tiles: bfloat16 [1024, 256, 256], P('state'), may hold values from 0 to 1
- tile_src: int32 [1024], P('state'), may hold values from 0 to 127, as said below
- tile_dst: int32 [1024], P('state'), may hold values from 0 to 127, as said below
- tile_action: int32 [1024], P('state'), may hold values from 0 to 7, as said below
- obs_prob: bfloat16 [8, 32, 32768], P(None, None, 'state'), may hold values from 0.049804688 to 1
- action_index: int32 [2048], P('vec'), may hold values from 0 to 7
- obs_index: int32 [2048], P('vec'), may hold values from 0 to 31
- alphas: bfloat16 [2048, 32768], P('vec', 'state'), may hold values from -1536 to 1536
Outputs:
- new_belief: bfloat16 [2048, 32768], P('vec', 'state')
- value: float32 [2048], P(('vec', 'state'))
Inputs may be any that keep to these rules, and one draw needn't show every extreme that they name: `tile_dst`: the slots of index j of state, slots j * 64 to (j + 1) * 64 - 1, name destination tiles j * 8 to (j + 1) * 8 - 1. `tile_action`: each index of state holds exactly 8 slots of every action. `tile_src`: among the slots of any one action, every source tile is named exactly once.
All inputs are finite; a program needn't handle non-finite values.
Results may differ from a plain program's by a relative error of at most 0.0015.
Values may be sent and summed in bfloat16 or wider, within the bound.
A program may use at most 128 MiB of HBM per device.

v0:
```python
import jax
import jax.numpy as jnp
from jax import lax
from jax.sharding import PartitionSpec as P

TILE = 256
ACT = 8
OBS = 32


def per_device(
    beliefs, tiles, tile_src, tile_dst, tile_action, obs_prob, action_index, obs_index, alphas
):
    shard_id = lax.axis_index("state")
    count_state = lax.axis_size("state")
    count_vec = lax.axis_size("vec")
    bel_rows, state_cols = beliefs.shape
    tiles_here = state_cols // TILE
    gathered = lax.all_gather(beliefs, "state", axis=1, tiled=True)
    sources = jnp.take(gathered.reshape(bel_rows, -1, TILE), tile_src, axis=1)
    contrib = jnp.einsum("btk,tkc->tbc", sources, tiles, preferred_element_type=jnp.float32)
    act_mask = (tile_action[:, None] == action_index[None, :]).astype(jnp.float32)
    masked = contrib * act_mask[:, :, None]
    local_dst = tile_dst - shard_id * tiles_here
    dst_onehot = (local_dst[None, :] == jnp.arange(tiles_here, dtype=jnp.int32)[:, None]).astype(
        jnp.float32
    )
    placed = jnp.einsum("dt,tbc->dbc", dst_onehot, masked, precision=lax.Precision.HIGHEST)
    reached = jnp.transpose(placed, (1, 0, 2)).reshape(bel_rows, state_cols)
    obs_codes = action_index * OBS + obs_index
    code_onehot = (obs_codes[:, None] == jnp.arange(ACT * OBS, dtype=jnp.int32)[None, :]).astype(
        jnp.bfloat16
    )
    obs_rows = jnp.dot(
        code_onehot, obs_prob.reshape(ACT * OBS, state_cols), preferred_element_type=jnp.float32
    )
    unnorm = reached * obs_rows
    totals = lax.psum(jnp.sum(unnorm, axis=1), "state")
    states_all = float(state_cols * count_state)
    new_belief = (states_all * unnorm / totals[:, None]).astype(jnp.bfloat16)
    rows_each = bel_rows // count_state
    partial_scores = lax.dot_general(
        lax.all_gather(new_belief, "vec", axis=0, tiled=True),
        alphas,
        (((1,), (1,)), ((), ())),
        preferred_element_type=jnp.float32,
    )
    ordered = partial_scores.reshape(count_vec, count_state, rows_each, -1)
    ordered = jnp.transpose(ordered, (1, 0, 2, 3)).reshape(count_vec * bel_rows, -1)
    summed = lax.psum_scatter(ordered, "state", scatter_dimension=0, tiled=True)
    best_rows = jnp.max(summed.reshape(count_vec, rows_each, -1), axis=2)
    best_rows = lax.pmax(best_rows, "vec")
    value_rows = lax.dynamic_index_in_dim(best_rows, lax.axis_index("vec"), 0, keepdims=False)
    return (new_belief, value_rows / states_all)


def solution(mesh):
    placed = (
        P("vec", "state"),
        P("state", None, None),
        P("state"),
        P("state"),
        P("state"),
        P(None, None, "state"),
        P("vec"),
        P("vec"),
        P("vec", "state"),
    )
    return jax.shard_map(
        per_device,
        mesh=mesh,
        in_specs=placed,
        out_specs=(P("vec", "state"), P(("vec", "state"))),
        check_vma=False,
    )
```

profile of v0, /device:TPU:1, one launch (start us, length us, event | category | flops | bytes accessed | tf_op | source)
XLA Modules:
  0.0 388.3 jit_solution(4000554093282682157)
XLA Ops:
  7.2 0.0 copy-start
  7.2 0.0 all-gather.3.cloned.1.call-start
  7.2 2.1 copy.12
  9.3 0.0 all-gather.3.cloned.1.call-update
  9.4 0.0 all-gather.5.cloned.1.call-start
  9.4 0.7 compare_select_fusion
  10.1 0.7 compare_and_fusion
  10.8 0.7 broadcast_subtract_fusion
  11.4 0.7 multiply_add_fusion
  12.1 0.7 compare_convert_fusion
  12.8 105.5 %all-gather.3.cloned.1.call-done = bf16[128,32768]{0,1:T(8,128)(2,1)} async-done(((bf16[128,2048]{0,1:T(8,128)(2,1)}), bf16[128,32768]{0,1:T(8,128)(2,1)}) %all-gather.3.cloned.1.call-update) | async-done | bytes 8388624 | tf_op jit(solution)/shard_map/all_gather | solution.py:19
  118.3 11.9 %copy.13 = bf16[128,128,256]{2,0,1:T(8,128)(2,1)} copy(bf16[128,128,256]{0,2,1:T(8,128)(2,1)} %bitcast.24) | data formatting | bytes 16777216 | tf_op jit(solution)/shard_map/reshape | solution.py:20
  130.2 6.2 %gather_fusion = bf16[64,128,256]{2,1,0:T(8,128)(2,1)} fusion(bf16[128,128,256]{2,0,1:T(8,128)(2,1)} %copy.13, s32[1024]{0:T(1024)S(1)} %pad_clamp_fusion), kind=kCustom, calls=%fused_computation | custom fusion | bytes 8388864 | tf_op jit(solution)/shard_map/jit(_take)/gather | solution.py:20
  136.4 5.4 %broadcast_multiply_fusion = f32[64,128,256]{2,1,0:T(8,128)S(1)} fusion(f32[64,128]{1,0:T(8,128)S(1)} %compare_convert_fusion, bf16[64,256,256]{2,1,0:T(8,128)(2,1)} %param.10, bf16[64,128,256]{2,1,0:T(8,128)(2,1)} %gather_fusion, pred[64]{0:T(512)(128)(4,1)S(1)} %compare_and_fusion), kind=kOutput, calls=%fused_computation.6 | convolution fusion | flops 1077936128 | bytes 21004352 | tf_op jit(solution)/shard_map/btk,tkc->tbc/dot_general | solution.py:21
  141.8 0.0 copy-start.1
  141.9 7.5 %fusion = f32[8,128,256]{2,0,1:T(8,128)S(1)} fusion(f32[64,128,256]{2,1,0:T(8,128)S(1)} %broadcast_multiply_fusion, s32[64]{0:T(128)S(1)} %broadcast_subtract_fusion), kind=kOutput, calls=%fused_computation.1 | convolution fusion | flops 201327104 | bytes 9437440 | tf_op jit(solution)/shard_map/dt,tbc->dbc/dot_general | solution.py:28
  149.3 0.3 copy.16
  149.7 0.0 copy-done
  149.7 0.4 fusion.14
  150.1 50.5 %psum.7 = f32[128]{0:T(128)S(1)} all-reduce(f32[128]{0:T(128)S(1)} %get-tuple-element.2), channel_id=1, replica_groups=mesh['vec'=16,'state'=16] {'state'}, use_global_device_ids=true, to_apply=%region_1.2 | all-reduce | flops 128 | bytes 1024 | tf_op jit(solution)/shard_map/psum | solution.py:38
  200.6 1.0 divide_convert_fusion
  201.6 0.0 all-gather.5.cloned.1.call-update
  201.6 0.2 reduce-scatter.2.cloned.1.call-start
  201.8 55.8 %all-gather.5.cloned.1.call-done = bf16[2048,2048]{1,0:T(8,128)(2,1)} async-done(((bf16[128,2048]{1,0:T(8,128)(2,1)}), bf16[2048,2048]{1,0:T(8,128)(2,1)}) %all-gather.5.cloned.1.call-update) | async-done | bytes 8388624 | tf_op jit(solution)/shard_map/all_gather | solution.py:43
  257.7 0.0 copy-done.1
  257.7 5.8 %fusion.15 = f32[2048,128]{1,0:T(8,128)S(1)} fusion(bf16[2048,2048]{1,0:T(8,128)(2,1)} %all-gather.5.cloned.1.call-done, bf16[128,2048]{1,0:T(8,128)(2,1)S(1)} %copy-done.1), kind=kOutput, calls=%fused_computation.25 | convolution fusion | flops 1073741824 | bytes 9961472 | tf_op jit(solution)/shard_map/dot_general | solution.py:42
  263.4 1.1 copy.15
  264.5 0.0 reduce-scatter.2.cloned.1.call-update
  264.6 86.0 %reduce-scatter.2.cloned.1.call-done = f32[128,128]{1,0:T(8,128)} async-done(((f32[2048,128]{1,0:T(8,128)}), f32[128,128]{1,0:T(8,128)}) %reduce-scatter.2.cloned.1.call-update) | async-done | bytes 65552 | tf_op jit(solution)/shard_map/reduce_scatter | solution.py:50
  350.5 0.9 reduce_max.11
  351.5 0.1 reduce_max.12
  351.6 29.6 %pmax.7 = f32[16,8]{1,0:T(8,128)S(1)} all-reduce(f32[16,8]{1,0:T(8,128)S(1)} %reduce_max.12), channel_id=1, replica_groups=mesh['vec'=16,'state'=16] {'vec'}, use_global_device_ids=true, to_apply=%region_4.5 | all-reduce | flops 128 | bytes 1024 | tf_op jit(solution)/shard_map/pmax | solution.py:52
  381.2 0.5 multiply_bitcast_fusion
  (1 shorter events, 0.0 us)
Async XLA Ops:
  7.2 142.5 %copy-start = (bf16[8,32,2048]{2,1,0:T(8,128)(2,1)S(1)}, bf16[8,32,2048]{2,1,0:T(8,128)(2,1)}, u32[]{:S(2)}) copy-start(bf16[8,32,2048]{2,1,0:T(8,128)(2,1)} %param.14) | copy-start | bytes 3145732
  7.2 111.1 %all-gather.3.cloned.1.call-start = ((), (), s32[]{:S(2)}) async-start(), calls=%async_computation.1 | async-start | bytes 8912896 | tf_op jit(solution)/shard_map/all_gather | solution.py:19
  9.4 248.3 %all-gather.5.cloned.1.call-start = ((), (), s32[]{:S(2)}) async-start(), calls=%async_computation.2 | async-start | bytes 8912896 | tf_op jit(solution)/shard_map/all_gather | solution.py:43
  141.8 115.8 %copy-start.1 = (bf16[128,2048]{1,0:T(8,128)(2,1)S(1)}, bf16[128,2048]{1,0:T(8,128)(2,1)}, u32[]{:S(2)}) copy-start(bf16[128,2048]{1,0:T(8,128)(2,1)} %param.17) | copy-start | bytes 1572868
  201.6 149.0 %reduce-scatter.2.cloned.1.call-start = ((), (), s32[]{:S(2)}) async-start(), calls=%async_computation.3 | async-start | bytes 1114112 | tf_op jit(solution)/shard_map/reduce_scatter | solution.py:50
Sparse Core Ops, SparseCore 0:
  11.0 107.2 all-gather.2
  201.7 55.8 all-gather.4
  264.7 85.8 reduce-scatter.1
where the time goes:
time: 389 us; the launch traced here: 388 us
  waiting for transfers between devices  247 us (63%)
  blocking collectives  80.1 us (21%)
  local copies, waits for them, and re-layouts  21.8 us (6%)
  matrix products  19.1 us (5%)
  between operations  13.8 us (4%)
  other arithmetic  5.83 us (1%)
    all_gather x1, waiting for transfers between devices, per_device(): gathered = lax.all_gather(beliefs, 'state', axis=1, tiled=True)  105 us
    reduce_scatter x1, waiting for transfers between devices, per_device(): summed = lax.psum_scatter(ordered, 'state', scatter_dimension=0, tiled=True)  86 us
    all_gather x1, waiting for transfers between devices, per_device(): lax.all_gather(new_belief, 'vec', axis=0, tiled=True)  55.8 us
    psum x1, blocking collectives, per_device(): totals = lax.psum(jnp.sum(unnorm, axis=1), 'state')  50.5 us
    pmax x1, blocking collectives, per_device(): best_rows = lax.pmax(best_rows, 'vec')  29.6 us
    reshape x1, local copies, waits for them, and re-layouts, per_device(): sources = jnp.take(gathered.reshape(bel_rows, -1, TILE), tile_src, axis=1)  11.9 us
  transfers between devices with their start and end apart: 3, of which 3 were waited for; matrix products, arithmetic and copies ran while one was open for 1% of the time, Pallas kernels for 0%

commit v1 on v0

v1 whole, which is shorter than its diff:
```python
import functools

import jax
import jax.numpy as jnp
from jax import lax
from jax.experimental import pallas as pl
from jax.experimental.pallas import tpu as pltpu
from jax.sharding import PartitionSpec as P

TILE = 256
ACT = 8
OBS = 32
KS = 8
NX = 4
NZ = 4
PIECES = 4
MESH = pl.DeviceIdType.MESH
F32 = jnp.float32
BF16 = jnp.bfloat16


def remote(src, dst, send, recv, dev):
    return pltpu.make_async_remote_copy(
        src_ref=src, dst_ref=dst, send_sem=send, recv_sem=recv, device_id=dev, device_id_type=MESH
    )


def greet(devs):
    barrier = pltpu.get_barrier_semaphore()
    for dev in devs:
        pl.semaphore_signal(barrier, inc=1, device_id=dev, device_id_type=MESH)
    pl.semaphore_wait(barrier, len(devs))


def exchange_kernel(
    tab_ref, act_ref, bel_ref, alp_ref, out_ref, all_ref,
    g0_ref, g1_ref, g2_ref, g3_ref, pick_ref, land_ref, tabs_ref, smem_ref, mask_ref,
    bel_sem, loc_sem, tab_send, tab_recv, tab_loc, z_send, z_recv, f_send, f_recv, x_send, x_recv,
    b_send, b_recv,
):
    v = lax.axis_index("vec")
    s = lax.axis_index("state")
    x, zh = s // NZ, s % NZ
    y, zl, core = v // 4, (v // 2) % 2, v % 2
    rows = bel_ref.shape[0]
    rp = rows // PIECES

    def at_state(xx, zz):
        return (v, xx * NZ + zz)

    def at_vec(yy, ll, cc):
        return (yy * 4 + ll * 2 + cc, s)

    z_dev = [at_state(x, (zh + 1) % NZ), at_state(x, (zh + 3) % NZ)]
    x_dev = [at_state((x + j) % NX, zh) for j in range(1, NX)]
    y_dev = [at_vec((y + 1) % 4, zl, core), at_vec((y + 3) % 4, zl, core)]
    pair_dev = at_vec(y, 1 - zl, core)
    sib_dev = at_vec(y, zl, 1 - core)

    g_refs = [g0_ref, g1_ref, g2_ref, g3_ref]
    own_bel = {}
    for p in range(PIECES):
        for t in range(KS):
            own_bel[p, t] = pltpu.make_async_copy(
                bel_ref.at[pl.ds(p * rp, rp), pl.ds(t * TILE, TILE)],
                g_refs[p].at[zh * KS + t], bel_sem.at[p, t],
            )
            own_bel[p, t].start()
    own_tab = pltpu.make_async_copy(tab_ref, smem_ref.at[0], loc_sem.at[2])
    own_tab.start()
    own_alp = pltpu.make_async_copy(alp_ref, all_ref.at[v], loc_sem.at[1])
    own_alp.start()
    greet(z_dev + x_dev + y_dev + [pair_dev, sib_dev])
    for c in own_bel.values():
        c.wait()

    tab_copies = []
    for j in range(1, NX):
        c = remote(tab_ref, tabs_ref.at[j], tab_send.at[j], tab_recv.at[j], x_dev[j - 1])
        c.start()
        tab_copies.append(c)

    def own_send(p, d):
        part = g_refs[p].at[pl.ds(zh * KS, KS)]
        return remote(part, part, z_send.at[d, p], z_recv.at[d, p], z_dev[d])

    def forward(p, d):
        origin = (zh + 3) % NZ if d == 0 else (zh + 1) % NZ
        part = g_refs[p].at[pl.ds(origin * KS, KS)]
        return remote(part, part, f_send.at[p], f_recv.at[p], z_dev[d])

    sends = []

    def go(c):
        c.start()
        sends.append(c)
        return c

    own = {}
    for p in range(2):
        for d in range(2):
            own[p, d] = go(own_send(p, d))

    n_b = [0]

    def b_copy(src, dst, dev):
        i = n_b[0]
        n_b[0] += 1
        return go(remote(src, dst, b_send.at[i], b_recv.at[i], dev))

    half = rows // 2

    def block(yy, ll, lo=0, n=rows):
        return all_ref.at[yy * 4 + ll * 2 + core, pl.ds(lo, n)]

    mine = all_ref.at[v]
    b_up = b_copy(alp_ref, mine, y_dev[0])
    b_down = b_copy(alp_ref, mine, y_dev[1])
    b_pair = b_copy(alp_ref, mine, pair_dev)
    b_sib = [b_copy(alp_ref, mine, sib_dev)]
    stage = {}

    def ring_forward(name, ll, up, down):
        up.wait_recv()
        lo = block((y + 3) % 4, ll, 0, half)
        stage[name, 0] = b_copy(lo, lo, y_dev[0])
        down.wait_recv()
        hi = block((y + 1) % 4, ll, half, half)
        stage[name, 1] = b_copy(hi, hi, y_dev[1])
        for yy in ((y + 3) % 4, (y + 1) % 4):
            whole = block(yy, ll)
            b_sib.append(b_copy(whole, whole, sib_dev))

    def ring_end(name, ll):
        stage[name, 0].wait_recv()
        stage[name, 1].wait_recv()
        whole = block((y + 2) % 4, ll)
        b_sib.append(b_copy(whole, whole, sib_dev))

    mask_ref[...] = jnp.zeros_like(mask_ref)
    for a in range(ACT):
        hit = jnp.where(act_ref[...] == a, 1.0, 0.0).astype(F32)
        hit = jnp.broadcast_to(hit, (rows, TILE)).astype(BF16)
        for p in range(PIECES):
            mask_ref[(p * ACT + a) * NX] = hit[p * rp : (p + 1) * rp]

    for c in tab_copies:
        c.wait()
    to_smem = pltpu.make_async_copy(tabs_ref.at[pl.ds(1, NX - 1)], smem_ref.at[pl.ds(1, NX - 1)], tab_loc)
    to_smem.start()
    to_smem.wait()
    own_tab.wait()

    def pick(j, p, into):
        def one(k, carry):
            acc = None
            for a in range(ACT):
                src = smem_ref[(NX - j) % NX, 0, a * KS + k]
                tile = g_refs[p][src & (NZ * KS - 1)]
                away = ((src >> 5) + NX - x) & (NX - 1)
                m = mask_ref[(p * ACT + a) * NX + away]
                acc = tile * m if acc is None else acc + tile * m
            into[k, pl.ds(p * rp, rp)] = acc
            return carry

        lax.fori_loop(0, KS, one, 0)

    fwd = {}
    x_copies = []
    partner = 1 - zl
    later = {}
    for p in range(PIECES):
        own[p, 0].wait_recv()
        if p % 2 == 0:
            fwd[p] = go(forward(p, 0))
        own[p, 1].wait_recv()
        if p % 2 == 1:
            fwd[p] = go(forward(p, 1))
        if p + 2 < PIECES:
            for d in range(2):
                own[p + 2, d] = go(own_send(p + 2, d))
        if p == 0:
            ring_forward(0, zl, b_up, b_down)
        if p == 1:
            ring_end(0, zl)
            b_pair.wait_recv()
            whole = block(y, partner)
            later[0] = b_copy(whole, whole, y_dev[0])
            later[1] = b_copy(whole, whole, y_dev[1])
            b_sib.append(b_copy(whole, whole, sib_dev))
        if p == 2:
            ring_forward(1, partner, later[0], later[1])
        fwd[p].wait_recv()
        for j in range(1, NX):
            pick(j, p, pick_ref.at[j])
            part = pl.ds(p * rp, rp)
            x_copies.append(
                go(remote(
                    pick_ref.at[j, :, part], land_ref.at[j, :, part],
                    x_send.at[j, p], x_recv.at[j, p], x_dev[j - 1],
                ))
            )
        pick(0, p, land_ref.at[0])
    ring_end(1, partner)

    for c in x_copies:
        c.wait_recv()

    def merge(k, carry):
        out_ref[k] = (land_ref[0, k] + land_ref[1, k]) + (land_ref[2, k] + land_ref[3, k])
        return carry

    lax.fori_loop(0, KS, merge, 0)
    own_alp.wait()
    for c in b_sib:
        c.wait_recv()
    for c in sends:
        c.wait_send()


def exchange(tab, act, beliefs, alphas, n_vec):
    rows, cols = beliefs.shape
    dma = pltpu.SemaphoreType.DMA
    vmem = pl.BlockSpec(memory_space=pltpu.VMEM)
    return pl.pallas_call(
        exchange_kernel,
        out_shape=(
            jax.ShapeDtypeStruct((KS, rows, TILE), BF16),
            jax.ShapeDtypeStruct((n_vec, rows, cols), BF16),
        ),
        in_specs=[vmem, vmem, pl.BlockSpec(memory_space=pl.ANY), vmem],
        out_specs=(vmem, pl.BlockSpec(memory_space=pl.ANY)),
        scratch_shapes=[
            *[pltpu.VMEM((NZ * KS, rows // PIECES, TILE), BF16)] * PIECES,
            pltpu.VMEM((NX, KS, rows, TILE), BF16),
            pltpu.VMEM((NX, KS, rows, TILE), BF16),
            pltpu.VMEM((NX, 8, 128), jnp.int32),
            pltpu.SMEM((NX, 8, 128), jnp.int32),
            pltpu.VMEM((PIECES * ACT * NX, rows // PIECES, TILE), BF16),
            dma((PIECES, KS)), dma((3,)), dma((NX,)), dma((NX,)), dma(()),
            dma((2, PIECES)), dma((2, PIECES)), dma((PIECES,)), dma((PIECES,)),
            dma((NX, PIECES)), dma((NX, PIECES)), dma((20,)), dma((20,)),
        ],
        compiler_params=pltpu.CompilerParams(
            collective_id=0, has_side_effects=True, vmem_limit_bytes=40 << 20
        ),
    )(tab, act, beliefs, alphas)


def tiles_kernel(
    sact_ref, rank_ref, dst_ref, act_ref, code_ref, src_ref, tiles_ref, obs_ref,
    unnorm_ref, u_ref, tot_ref, acc_ref, mask_ref,
):
    step = pl.program_id(0)
    per = tiles_ref.shape[0]
    rows = src_ref.shape[1]

    @pl.when(step == 0)
    def _():
        acc_ref[...] = jnp.zeros_like(acc_ref)
        for a in range(ACT):
            hit = jnp.where(act_ref[...] == a, 1.0, 0.0).astype(F32)
            mask_ref[a] = jnp.broadcast_to(hit, (rows, TILE)).astype(BF16)

    for i in range(per):
        t = step * per + i
        left = src_ref[rank_ref[t]] * mask_ref[sact_ref[t]]
        part = jnp.dot(left, tiles_ref[i], preferred_element_type=F32)
        d = dst_ref[t]
        acc_ref[d] = acc_ref[d] + part

    @pl.when(step == pl.num_programs(0) - 1)
    def _():
        codes = lax.broadcasted_iota(jnp.int32, (rows, ACT * OBS), 1)
        hot = jnp.where(code_ref[...] == codes, 1.0, 0.0).astype(BF16)
        total = jnp.zeros((rows, 1), F32)
        for d in range(acc_ref.shape[0]):
            cols = pl.ds(d * TILE, TILE)
            seen = jnp.dot(hot, obs_ref[:, cols], preferred_element_type=F32)
            un = acc_ref[d] * seen
            unnorm_ref[:, cols] = un
            u_ref[:, cols] = un.astype(BF16)
            total = total + jnp.sum(un, axis=1, keepdims=True)
        tot_ref[...] = jnp.transpose(jnp.broadcast_to(total, (rows, rows)))[:8]


def tile_products(sact, rank, dst, act, code, src, tiles, obs):
    _, rows, _ = src.shape
    nt = tiles.shape[0]
    cols = obs.shape[1]
    per = 8
    whole = pl.BlockSpec(memory_space=pltpu.VMEM)
    return pl.pallas_call(
        tiles_kernel,
        out_shape=(
            jax.ShapeDtypeStruct((rows, cols), F32),
            jax.ShapeDtypeStruct((rows, cols), BF16),
            jax.ShapeDtypeStruct((8, rows), F32),
        ),
        grid_spec=pltpu.PrefetchScalarGridSpec(
            num_scalar_prefetch=3,
            grid=(nt // per,),
            in_specs=[whole, whole, whole, pl.BlockSpec((per, TILE, TILE), lambda i, *_: (i, 0, 0)), whole],
            out_specs=[whole, whole, whole],
            scratch_shapes=[
                pltpu.VMEM((cols // TILE, rows, TILE), F32),
                pltpu.VMEM((ACT, rows, TILE), BF16),
            ],
        ),
        compiler_params=pltpu.CompilerParams(vmem_limit_bytes=40 << 20),
    )(sact, rank, dst, act, code, src, tiles, obs)


NB = 8


def score_kernel(
    scale, unnorm_ref, u_ref, tot_ref, all_ref, new_ref, val_ref,
    b_ref, c_ref, xr_ref, d_ref, zr_ref, tots_ref, tcol_ref,
    ld_sem, t_send, t_recv, x_send, x_recv, z_send, z_recv,
):
    v = lax.axis_index("vec")
    s = lax.axis_index("state")
    x, zh = s // NZ, s % NZ
    rows = u_ref.shape[0]
    wide = b_ref.shape[1]
    n_state = NX * NZ

    loads = []
    for n in range(NB):
        c = pltpu.make_async_copy(all_ref.at[pl.ds(n * wide, wide)], b_ref.at[n], ld_sem.at[n])
        c.start()
        loads.append(c)

    peers = [(v, (s + i) % n_state) for i in range(1, n_state)]
    greet(peers)

    sends = []

    def go(c):
        c.start()
        sends.append(c)
        return c

    tot_copies = [
        go(remote(tot_ref, tots_ref.at[i], t_send.at[i], t_recv.at[i], peers[i - 1]))
        for i in range(1, n_state)
    ]
    tots_ref[0] = tot_ref[...]

    quarter = rows // NX
    x_copies = {}
    for n in range(NB):
        loads[n].wait()
        c_ref[n] = lax.dot_general(
            u_ref[...], b_ref[n], (((1,), (1,)), ((), ())), preferred_element_type=F32
        )
        for j in (2, 1, 3):
            xx = (x + j) % NX
            x_copies[n, j] = go(remote(
                c_ref.at[n, pl.ds(xx * quarter, quarter)], xr_ref.at[n, j],
                x_send.at[n, j], x_recv.at[n, j], (v, xx * NZ + zh),
            ))

    for c in tot_copies:
        c.wait_recv()
    total = jnp.zeros((8, rows), F32)
    for q in range(n_state):
        total = total + tots_ref[(s + n_state - q) % n_state]
    tcol_ref[...] = jnp.transpose(jnp.broadcast_to(total[0:1], (rows, rows)))

    def norm(i, carry):
        cols = pl.ds(pl.multiple_of(i * rows, rows), rows)
        new_ref[:, cols] = ((scale * unnorm_ref[:, cols]) / tcol_ref[...]).astype(BF16)
        return carry

    lax.fori_loop(0, unnorm_ref.shape[1] // rows, norm, 0)

    each = quarter // NZ
    z_copies = {}
    for h in range(2):
        for n in range(h * NB // 2, (h + 1) * NB // 2):
            for j in range(1, NX):
                x_copies[n, j].wait_recv()
            mine = c_ref[n, pl.ds(pl.multiple_of(x * quarter, quarter), quarter)]
            d_ref[n] = (mine + xr_ref[n, 1]) + (xr_ref[n, 2] + xr_ref[n, 3])
        part = pl.ds(h * NB // 2, NB // 2)
        for j in (2, 1, 3):
            zz = (zh + j) % NZ
            z_copies[h, j] = go(remote(
                d_ref.at[part, pl.ds(zz * each, each)], zr_ref.at[j, part],
                z_send.at[h, j], z_recv.at[h, j], (v, x * NZ + zz),
            ))
    best = None
    for h in range(2):
        for j in range(1, NZ):
            z_copies[h, j].wait_recv()
        for n in range(h * NB // 2, (h + 1) * NB // 2):
            mine = d_ref[n, pl.ds(pl.multiple_of(zh * each, each), each)]
            full = (mine + zr_ref[1, n]) + (zr_ref[2, n] + zr_ref[3, n])
            best = full if best is None else jnp.maximum(best, full)
    top = jnp.max(best, axis=1, keepdims=True)
    mine = tcol_ref[pl.ds(pl.multiple_of(s * each, each), each)]
    val_ref[...] = jnp.broadcast_to(top, mine.shape) / mine
    for c in sends:
        c.wait_send()


def scores(unnorm, u, tot, alphas_all, scale):
    rows, cols = u.shape
    n_alpha = alphas_all.shape[0]
    wide = n_alpha // NB
    quarter = rows // NX
    n_state = NX * NZ
    dma = pltpu.SemaphoreType.DMA
    vmem = pl.BlockSpec(memory_space=pltpu.VMEM)
    return pl.pallas_call(
        functools.partial(score_kernel, scale),
        out_shape=(
            jax.ShapeDtypeStruct((rows, cols), BF16),
            jax.ShapeDtypeStruct((rows // n_state, rows), F32),
        ),
        in_specs=[vmem, vmem, vmem, pl.BlockSpec(memory_space=pl.ANY)],
        out_specs=(vmem, vmem),
        scratch_shapes=[
            pltpu.VMEM((NB, wide, cols), BF16),
            pltpu.VMEM((NB, rows, wide), F32),
            pltpu.VMEM((NB, NX, quarter, wide), F32),
            pltpu.VMEM((NB, quarter, wide), F32),
            pltpu.VMEM((NZ, NB, quarter // NZ, wide), F32),
            pltpu.VMEM((n_state, 8, rows), F32),
            pltpu.VMEM((rows, rows), F32),
            dma((NB,)), dma((n_state,)), dma((n_state,)),
            dma((NB, NX)), dma((NB, NX)), dma((2, NZ)), dma((2, NZ)),
        ],
        compiler_params=pltpu.CompilerParams(
            collective_id=1, has_side_effects=True, vmem_limit_bytes=40 << 20
        ),
    )(unnorm, u, tot, alphas_all)


def per_device(
    beliefs, tiles, tile_src, tile_dst, tile_action, obs_prob, action_index, obs_index, alphas
):
    shard_id = lax.axis_index("state")
    n_vec = lax.axis_size("vec")
    n_state = lax.axis_size("state")
    rows, cols = beliefs.shape
    nt = tile_src.shape[0]
    slots = jnp.arange(nt, dtype=jnp.int32)
    earlier = (tile_action[None, :] == tile_action[:, None]) & (slots[None, :] < slots[:, None])
    rank = jnp.sum(earlier.astype(jnp.int32), axis=1)
    place = tile_action * KS + rank
    lanes = jnp.arange(128, dtype=jnp.int32)
    table = jnp.sum(jnp.where(place[:, None] == lanes[None, :], tile_src[:, None], 0), axis=0)
    table = jnp.broadcast_to(table[None, :], (8, 128)).astype(jnp.int32)
    act_col = action_index[:, None]
    code_col = (action_index * OBS + obs_index)[:, None]
    local_dst = tile_dst - shard_id * (cols // TILE)

    src, alphas_all = exchange(table, act_col, beliefs, alphas, n_vec)
    unnorm, u, tot = tile_products(
        tile_action, rank, local_dst, act_col, code_col, src, tiles, obs_prob.reshape(ACT * OBS, cols)
    )
    new_belief, value = scores(
        unnorm, u, tot, alphas_all.reshape(n_vec * rows, cols), float(cols * n_state)
    )
    return new_belief, value[:, 0]


def solution(mesh):
    placed = (
        P("vec", "state"),
        P("state", None, None),
        P("state"),
        P("state"),
        P("state"),
        P(None, None, "state"),
        P("vec"),
        P("vec"),
        P("vec", "state"),
    )
    return jax.shard_map(
        per_device,
        mesh=mesh,
        in_specs=placed,
        out_specs=(P("vec", "state"), P(("vec", "state"))),
        check_vma=False,
    )
```

time: 389 us -> 116 us (0.30)
  waiting for transfers between devices: 247 us -> 0 us
  Pallas kernels: 0 us -> 101 us
  blocking collectives: 80.1 us -> 0 us
  matrix products: 19.1 us -> 0 us
  between operations: 13.8 us -> 0.68 us
  local copies, waits for them, and re-layouts: 21.8 us -> 9.63 us
    all_gather x2 -> x0, waiting for transfers between devices: 161 us -> none  [the longest x1 105 us: per_device(): gathered = lax.all_gather(beliefs, 'state', axis=1, tiled=True)]
    pallas_call x0 -> x3, Pallas kernels: none -> 101 us  [the longest x1 71.5 us: exchange(): pl.pallas_call(exchange_kernel, out_shape=(jax.ShapeDtypeStruct((KS, rows...]
    reduce_scatter x1 -> x0, waiting for transfers between devices: 86 us -> none  [per_device(): summed = lax.psum_scatter(ordered, 'state', scatter_dimension=0, tiled=True)]
    psum x1 -> x0, blocking collectives: 50.5 us -> none  [per_device(): totals = lax.psum(jnp.sum(unnorm, axis=1), 'state')]
    pmax x1 -> x0, blocking collectives: 29.6 us -> none  [per_device(): best_rows = lax.pmax(best_rows, 'vec')]
    dot_general x4 -> x0, matrix products: 19.1 us -> none  [the longest x1 7.49 us: per_device(): jnp.einsum('dt,tbc->dbc', dst_onehot, masked, precision=lax.Precision.HIG...]
    reshape x2 -> x0, local copies, waits for them, and re-layouts: 13 us -> none  [the longest x1 11.9 us: per_device(): sources = jnp.take(gathered.reshape(bel_rows, -1, TILE), tile_src, axis=1)]
    gather x1 -> x0, local copies, waits for them, and re-layouts: 6.17 us -> none  [per_device(): sources = jnp.take(gathered.reshape(bel_rows, -1, TILE), tile_src, axis=1)]
  transfers between devices with their start and end apart: 3 -> 0, of which waited for: 3 -> 0; matrix products, arithmetic and copies ran while one was open for 1% -> 0% of each run, Pallas kernels for 0% -> 0%
where the time goes in v1:
time: 116 us; the launch traced here: 115 us
  Pallas kernels  101 us (87%)
  local copies, waits for them, and re-layouts  9.63 us (8%)
  other arithmetic  3.66 us (3%)
    pallas_call x1, Pallas kernels, exchange(): pl.pallas_call(exchange_kernel, out_shape=(jax.ShapeDtypeStruct((KS, rows...  71.5 us
    pallas_call x1, Pallas kernels, scores(): pl.pallas_call(functools.partial(score_kernel, scale), out_shape=(jax.Sha...  25.1 us
    unnamed x11, local copies, waits for them, and re-layouts  8.13 us
    pallas_call x1, Pallas kernels, tile_products(): pl.pallas_call(tiles_kernel, out_shape=(jax.ShapeDtypeStruct((rows, cols)...  3.98 us

profile of v1, /device:TPU:1, one launch (start us, length us, event | category | flops | bytes accessed | tf_op | source)
XLA Modules:
  0.0 114.5 jit_solution(8676431604711428071)
XLA Ops:
  0.6 0.7 broadcast_subtract_fusion.dst_ref
  1.3 0.9 convert_reduce_fusion.rank_ref
  2.2 0.7 multiply_add_fusion
  2.9 0.7 select_reduce_fusion
  3.6 0.7 add_bitcast_fusion
  4.3 0.1 copy.19.code_ref
  4.4 0.8 copy.18.act_ref
  5.2 0.0 copy-start.2
  5.2 1.0 copy-done.2
  6.2 0.0 copy-start.3
  6.2 1.0 copy-done.3
  7.3 71.5 %shard_map.104 = (bf16[8,128,256]{2,1,0:T(8,128)(2,1)S(1)}, bf16[16,128,2048]{2,1,0:T(8,128)(2,1)S(1)}) custom-call(s32[8,128]{1,0:T(8,128)S(1)} %broadcast_in_dim.35.tab_ref, s32[128,1]{1,0:T(8,128)S(1)} %copy.18.act_ref, bf16[128,2048]{1,0:T(8,128)(2,1)S(1)} %copy-done.2, bf16[128,2048]{1,0:T(8,128)(2,1)S(1)} %copy-done.3), custom_call_target="tpu_custom_call" | custom-call | tf_op jit(solution)/shard_map/pallas_call | solution.py:225
  78.8 0.0 copy-start
  78.8 3.4 %copy-done = bf16[64,256,256]{2,1,0:T(8,128)(2,1)S(1)} copy-done((bf16[64,256,256]{2,1,0:T(8,128)(2,1)S(1)}, bf16[64,256,256]{2,1,0:T(8,128)(2,1)}, u32[]{:S(2)}) %copy-start) | copy-done | bytes 8388632
  82.1 0.0 copy-start.1
  82.1 1.2 %copy-done.1 = bf16[8,32,2048]{2,1,0:T(8,128)(2,1)S(1)} copy-done((bf16[8,32,2048]{2,1,0:T(8,128)(2,1)S(1)}, bf16[8,32,2048]{2,1,0:T(8,128)(2,1)}, u32[]{:S(2)}) %copy-start.1) | copy-done | bytes 1048600
  83.4 0.0 copy-start.4
  83.4 0.7 copy-done.4
  84.0 4.0 %shard_map.105 = (f32[128,2048]{1,0:T(8,128)S(1)}, bf16[128,2048]{1,0:T(8,128)(2,1)S(1)}, f32[8,128]{1,0:T(8,128)S(1)}) custom-call(s32[64]{0:T(128)S(1)} %copy-done.4, s32[64]{0:T(128)S(1)} %convert_reduce_fusion.rank_ref, s32[64]{0:T(128)S(1)} %broadcast_subtract_fusion.dst_ref, s32[128,1]{1,0:T(8,128)S(1)} %copy.18.act_ref, s32[128,1]{1,0:T(8,128)S(1)} %copy.19.code_ref, ...), custom_call_target="tpu_custom_call" | custom-call | tf_op jit(solution)/shard_map/pallas_call | solution.py:293
  88.0 25.1 %shard_map.106 = (bf16[128,2048]{1,0:T(8,128)(2,1)S(1)}, f32[8,128]{1,0:T(8,128)S(1)}) custom-call(f32[128,2048]{1,0:T(8,128)S(1)} %get-tuple-element.10.unnorm_ref, bf16[128,2048]{1,0:T(8,128)(2,1)S(1)} %get-tuple-element.11.u_ref, f32[8,128]{1,0:T(8,128)S(1)} %get-tuple-element.12.tot_ref, bf16[2048,2048]{1,0:T(8,128)(2,1)S(1)} %bitcast.5), custom_call_target="tpu_custom_call" | custom-call | tf_op jit(solution)/shard_map/pallas_call | solution.py:417
  113.1 0.6 slice_reduce_fusion
  113.7 0.8 copy.21
  (1 shorter events, 0.0 us)
Async XLA Ops:
  5.2 1.0 copy-start.2
  6.2 1.0 copy-start.3
  78.8 3.4 %copy-start = (bf16[64,256,256]{2,1,0:T(8,128)(2,1)S(1)}, bf16[64,256,256]{2,1,0:T(8,128)(2,1)}, u32[]{:S(2)}) copy-start(bf16[64,256,256]{2,1,0:T(8,128)(2,1)} %tiles_ref.1) | copy-start | bytes 25165828
  82.1 1.2 %copy-start.1 = (bf16[8,32,2048]{2,1,0:T(8,128)(2,1)S(1)}, bf16[8,32,2048]{2,1,0:T(8,128)(2,1)}, u32[]{:S(2)}) copy-start(bf16[8,32,2048]{2,1,0:T(8,128)(2,1)} %param.14) | copy-start | bytes 3145732
  83.4 0.7 copy-start.4

commit v2 on v1

v2 whole, which is shorter than its diff:
```python
import functools

import jax
import jax.numpy as jnp
from jax import lax
from jax.experimental import pallas as pl
from jax.experimental.pallas import tpu as pltpu
from jax.sharding import PartitionSpec as P

TILE = 256
ACT = 8
OBS = 32
KS = 8
NX = 4
NZ = 4
PIECES = 4
MESH = pl.DeviceIdType.MESH
F32 = jnp.float32
BF16 = jnp.bfloat16


def remote(src, dst, send, recv, dev):
    return pltpu.make_async_remote_copy(
        src_ref=src, dst_ref=dst, send_sem=send, recv_sem=recv, device_id=dev, device_id_type=MESH
    )


def greet(devs):
    for dev in devs:
        pl.semaphore_signal(
            pltpu.get_barrier_semaphore(), inc=1, device_id=dev, device_id_type=MESH
        )


def all_here(devs):
    pl.semaphore_wait(pltpu.get_barrier_semaphore(), len(devs))


def exchange_kernel(
    tsrc_ref, tact_ref, act_ref, bel_ref, alp_ref, out_ref, all_ref,
    g0_ref, g1_ref, g2_ref, g3_ref, pick_ref, relay_ref, land_ref, tabs_ref, smem_ref, mask_ref,
    bel_sem, loc_sem, tab_send, tab_recv, z_send, z_recv, f_send, f_recv,
    r_send, r_recv, x_send, x_recv, b_send, b_recv,
):
    v = lax.axis_index("vec")
    s = lax.axis_index("state")
    x, zh = s // NZ, s % NZ
    y, zl, core = v // 4, (v // 2) % 2, v % 2
    rows = bel_ref.shape[0]
    rp = rows // PIECES
    kh = KS // 2

    def at_state(xx, zz):
        return (v, xx * NZ + zz)

    def at_vec(yy, ll, cc):
        return (yy * 4 + ll * 2 + cc, s)

    z_dev = [at_state(x, (zh + 1) % NZ), at_state(x, (zh + 3) % NZ)]
    x_dev = [at_state((x + j) % NX, zh) for j in range(1, NX)]
    y_dev = [at_vec((y + 1) % 4, zl, core), at_vec((y + 3) % 4, zl, core)]
    pair_dev = at_vec(y, 1 - zl, core)
    sib_dev = at_vec(y, zl, 1 - core)

    near = z_dev + x_dev + y_dev + [pair_dev, sib_dev]
    greet(near)
    g_refs = [g0_ref, g1_ref, g2_ref, g3_ref]
    own_bel = {}
    for p in range(PIECES):
        for t in range(KS):
            own_bel[p, t] = pltpu.make_async_copy(
                bel_ref.at[pl.ds(p * rp, rp), pl.ds(t * TILE, TILE)],
                g_refs[p].at[zh * KS + t], bel_sem.at[p, t],
            )
            own_bel[p, t].start()
    own_alp = pltpu.make_async_copy(alp_ref, all_ref.at[v], loc_sem.at[0])
    own_alp.start()

    nt = tact_ref.shape[1]
    act_l = jnp.broadcast_to(tact_ref[...].astype(F32), (nt, nt))
    act_s = jnp.transpose(act_l)
    src_s = jnp.transpose(jnp.broadcast_to(tsrc_ref[...].astype(F32), (nt, nt)))
    before = lax.broadcasted_iota(jnp.int32, (nt, nt), 1) < lax.broadcasted_iota(jnp.int32, (nt, nt), 0)
    rank = jnp.sum(jnp.where((act_l == act_s) & before, 1.0, 0.0), axis=1, keepdims=True)
    lane = lax.broadcasted_iota(jnp.int32, (nt, 128), 1).astype(F32)
    by_rank = jnp.where(rank == lane, 1.0, 0.0)
    by_act = jnp.where(act_s[:, :1] == lane, src_s[:, :1], 0.0)
    table = lax.dot_general(
        by_rank.astype(BF16), by_act.astype(BF16), (((0,), (0,)), ((), ())), preferred_element_type=F32
    )
    tabs_ref[0] = table[:KS].astype(jnp.int32)

    mask_ref[...] = jnp.zeros_like(mask_ref)
    act_col = jnp.transpose(jnp.broadcast_to(act_ref[...].astype(F32), (rows, rows)))
    for a in range(ACT):
        hit = jnp.where(act_col == float(a), 1.0, 0.0).astype(BF16)
        for p in range(PIECES):
            for c in range(TILE // rows):
                mask_ref[(p * ACT + a) * NX, :, c * rows : (c + 1) * rows] = hit[p * rp : (p + 1) * rp]

    all_here(near)
    for c in own_bel.values():
        c.wait()

    sends = []

    def go(c):
        c.start()
        sends.append(c)
        return c

    def own_send(p, d):
        part = g_refs[p].at[pl.ds(zh * KS, KS)]
        return remote(part, part, z_send.at[d, p], z_recv.at[d, p], z_dev[d])

    def forward(p, d):
        origin = (zh + 3) % NZ if d == 0 else (zh + 1) % NZ
        part = g_refs[p].at[pl.ds(origin * KS + d * kh, kh)]
        return remote(part, part, f_send.at[d, p], f_recv.at[d, p], z_dev[d])

    own = {}
    for p in range(2):
        for d in range(2):
            own[p, d] = go(own_send(p, d))

    tab_copies = [
        go(remote(tabs_ref.at[0], tabs_ref.at[j], tab_send.at[j], tab_recv.at[j], x_dev[j - 1]))
        for j in range(1, NX)
    ]

    n_b = [0]

    def b_copy(src, dst, dev):
        i = n_b[0]
        n_b[0] += 1
        return go(remote(src, dst, b_send.at[i], b_recv.at[i], dev))

    half = rows // 2

    def block(yy, ll, lo=0, n=rows):
        return all_ref.at[yy * 4 + ll * 2 + core, pl.ds(lo, n)]

    mine = all_ref.at[v]
    b_up = b_copy(alp_ref, mine, y_dev[0])
    b_down = b_copy(alp_ref, mine, y_dev[1])
    b_pair = b_copy(alp_ref, mine, pair_dev)
    b_sib = [b_copy(alp_ref, mine, sib_dev)]
    stage = {}

    def ring_forward(name, ll, up, down):
        up.wait_recv()
        lo = block((y + 3) % 4, ll, 0, half)
        stage[name, 0] = b_copy(lo, lo, y_dev[0])
        down.wait_recv()
        hi = block((y + 1) % 4, ll, half, half)
        stage[name, 1] = b_copy(hi, hi, y_dev[1])
        for yy in ((y + 3) % 4, (y + 1) % 4):
            whole = block(yy, ll)
            b_sib.append(b_copy(whole, whole, sib_dev))

    def ring_end(name, ll):
        stage[name, 0].wait_recv()
        stage[name, 1].wait_recv()
        whole = block((y + 2) % 4, ll)
        b_sib.append(b_copy(whole, whole, sib_dev))

    for c in tab_copies:
        c.wait_recv()
    to_smem = pltpu.make_async_copy(tabs_ref, smem_ref, loc_sem.at[1])
    to_smem.start()
    to_smem.wait()

    def pick(j, p, into):
        def one(k, carry):
            acc = None
            for a in range(ACT):
                src = smem_ref[(NX - j) % NX, k, a]
                tile = g_refs[p][src & (NZ * KS - 1)]
                away = ((src >> 5) + NX - x) & (NX - 1)
                m = mask_ref[(p * ACT + a) * NX + away]
                acc = tile * m if acc is None else acc + tile * m
            into[k, pl.ds(p * rp, rp)] = acc
            return carry

        lax.fori_loop(0, KS, one, 0)

    fwd = {}
    x_copies = []

    def along_x(p):
        part = pl.ds(p * rp, rp)
        fwd[p, 0].wait_recv()
        fwd[p, 1].wait_recv()
        pick(2, p, pick_ref.at[0])
        relays = []
        for d in range(2):
            relays.append(go(remote(
                pick_ref.at[0, pl.ds(d * kh, kh), part], relay_ref.at[d, :, part],
                r_send.at[d, p], r_recv.at[d, p], x_dev[2 * d],
            )))
        pick(1, p, pick_ref.at[1])
        pick(3, p, pick_ref.at[2])
        pick(0, p, land_ref.at[0])
        for d in range(2):
            relays[d].wait_recv()
            for k in range(kh):
                pick_ref[1 + d, d * kh + k, part] = pick_ref[1 + d, d * kh + k, part] + relay_ref[d, k, part]
            x_copies.append(go(remote(
                pick_ref.at[1 + d, :, part], land_ref.at[1 + d, :, part],
                x_send.at[d, p], x_recv.at[d, p], x_dev[2 * d],
            )))

    partner = 1 - zl
    later = {}
    for p in range(PIECES):
        for d in range(2):
            own[p, d].wait_recv()
            fwd[p, d] = go(forward(p, d))
        if p + 2 < PIECES:
            for d in range(2):
                own[p + 2, d] = go(own_send(p + 2, d))
        if p == 1:
            ring_forward(0, zl, b_up, b_down)
        if p == 2:
            b_pair.wait_recv()
            whole = block(y, partner)
            later[0] = b_copy(whole, whole, y_dev[0])
            later[1] = b_copy(whole, whole, y_dev[1])
            b_sib.append(b_copy(whole, whole, sib_dev))
            ring_end(0, zl)
        if p:
            along_x(p - 1)
    ring_forward(1, partner, later[0], later[1])
    along_x(PIECES - 1)

    for c in x_copies:
        c.wait_recv()

    def merge(k, carry):
        out_ref[k] = (land_ref[0, k] + land_ref[1, k]) + land_ref[2, k]
        return carry

    lax.fori_loop(0, KS, merge, 0)
    ring_end(1, partner)
    own_alp.wait()
    for c in b_sib:
        c.wait_recv()
    for c in sends:
        c.wait_send()


BIG = 62 << 20


def exchange(tsrc, tact, act, beliefs, alphas, n_vec):
    rows, cols = beliefs.shape
    dma = pltpu.SemaphoreType.DMA
    vmem = pl.BlockSpec(memory_space=pltpu.VMEM)
    hbm = pl.BlockSpec(memory_space=pl.ANY)
    return pl.pallas_call(
        exchange_kernel,
        out_shape=(
            jax.ShapeDtypeStruct((KS, rows, TILE), BF16),
            jax.ShapeDtypeStruct((n_vec, rows, cols), BF16),
        ),
        in_specs=[vmem, vmem, vmem, hbm, hbm],
        out_specs=(vmem, hbm),
        scratch_shapes=[
            *[pltpu.VMEM((NZ * KS, rows // PIECES, TILE), BF16)] * PIECES,
            pltpu.VMEM((3, KS, rows, TILE), BF16),
            pltpu.VMEM((2, KS // 2, rows, TILE), BF16),
            pltpu.VMEM((3, KS, rows, TILE), BF16),
            pltpu.VMEM((NX, 8, 128), jnp.int32),
            pltpu.SMEM((NX, 8, 128), jnp.int32),
            pltpu.VMEM((PIECES * ACT * NX, rows // PIECES, TILE), BF16),
            dma((PIECES, KS)), dma((2,)), dma((NX,)), dma((NX,)),
            dma((2, PIECES)), dma((2, PIECES)), dma((2, PIECES)), dma((2, PIECES)),
            dma((2, PIECES)), dma((2, PIECES)), dma((2, PIECES)), dma((2, PIECES)),
            dma((20,)), dma((20,)),
        ],
        compiler_params=pltpu.CompilerParams(
            collective_id=0, has_side_effects=True, vmem_limit_bytes=BIG
        ),
    )(tsrc, tact, act, beliefs, alphas)


def tiles_kernel(
    sact_ref, dst_ref, act_ref, seen_ref, src_ref, tiles_ref, obs_ref,
    unnorm_ref, u_ref, tot_ref, acc_ref, mask_ref, count_ref,
):
    step = pl.program_id(0)
    per = tiles_ref.shape[0]
    rows = src_ref.shape[1]

    @pl.when(step == 0)
    def _():
        acc_ref[...] = jnp.zeros_like(acc_ref)
        act_col = jnp.transpose(jnp.broadcast_to(act_ref[...].astype(F32), (rows, rows)))
        for a in range(ACT):
            hit = jnp.where(act_col == float(a), 1.0, 0.0).astype(BF16)
            count_ref[a] = 0
            for c in range(TILE // rows):
                mask_ref[a, :, c * rows : (c + 1) * rows] = hit

    for i in range(per):
        t = step * per + i
        a = sact_ref[t]
        k = count_ref[a]
        count_ref[a] = k + 1
        left = src_ref[k] * mask_ref[a]
        part = jnp.dot(left, tiles_ref[i], preferred_element_type=F32)
        d = lax.rem(dst_ref[t], acc_ref.shape[0])
        acc_ref[d] = acc_ref[d] + part

    @pl.when(step == pl.num_programs(0) - 1)
    def _():
        code = act_ref[...] * OBS + seen_ref[...]
        codes = lax.broadcasted_iota(jnp.int32, (ACT * OBS, rows), 0)
        hot = jnp.where(codes == code, 1.0, 0.0).astype(BF16)
        total = jnp.zeros((rows, 1), F32)
        for d in range(acc_ref.shape[0]):
            cols = pl.ds(d * TILE, TILE)
            seen = lax.dot_general(
                hot, obs_ref[:, cols], (((0,), (0,)), ((), ())), preferred_element_type=F32
            )
            un = acc_ref[d] * seen
            unnorm_ref[:, cols] = un
            u_ref[:, cols] = un.astype(BF16)
            total = total + jnp.sum(un, axis=1, keepdims=True)
        tot_ref[...] = jnp.transpose(jnp.broadcast_to(total, (rows, rows)))[:8]


def tile_products(sact, dst, act, seen, src, tiles, obs):
    _, rows, _ = src.shape
    nt = tiles.shape[0]
    cols = obs.shape[1]
    per = 8
    whole = pl.BlockSpec(memory_space=pltpu.VMEM)
    return pl.pallas_call(
        tiles_kernel,
        out_shape=(
            jax.ShapeDtypeStruct((rows, cols), F32),
            jax.ShapeDtypeStruct((rows, cols), BF16),
            jax.ShapeDtypeStruct((8, rows), F32),
        ),
        grid_spec=pltpu.PrefetchScalarGridSpec(
            num_scalar_prefetch=2,
            grid=(nt // per,),
            in_specs=[whole, whole, whole, pl.BlockSpec((per, TILE, TILE), lambda i, *_: (i, 0, 0)), whole],
            out_specs=[whole, whole, whole],
            scratch_shapes=[
                pltpu.VMEM((cols // TILE, rows, TILE), F32),
                pltpu.VMEM((ACT, rows, TILE), BF16),
                pltpu.SMEM((ACT,), jnp.int32),
            ],
        ),
        compiler_params=pltpu.CompilerParams(vmem_limit_bytes=BIG),
    )(sact, dst, act, seen, src, tiles, obs)


NB = 8
GROUPS = 4


def score_kernel(
    scale, unnorm_ref, u_ref, tot_ref, all_ref, new_ref, val_ref,
    b_ref, c_ref, relay_ref, xr_ref, d_ref, zr_ref, tots_ref, tcol_ref,
    ld_sem, t_send, t_recv, r_send, r_recv, x_send, x_recv, z_send, z_recv,
):
    v = lax.axis_index("vec")
    s = lax.axis_index("state")
    x, zh = s // NZ, s % NZ
    rows = u_ref.shape[0]
    wide = b_ref.shape[1]
    n_state = NX * NZ

    loads = []
    for n in range(NB):
        c = pltpu.make_async_copy(all_ref.at[pl.ds(n * wide, wide)], b_ref.at[n], ld_sem.at[n])
        c.start()
        loads.append(c)

    peers = [(v, (s + i) % n_state) for i in range(1, n_state)]
    greet(peers)
    all_here(peers)

    sends = []

    def go(c):
        c.start()
        sends.append(c)
        return c

    tot_copies = [
        go(remote(tot_ref, tots_ref.at[i], t_send.at[i], t_recv.at[i], peers[i - 1]))
        for i in range(1, n_state)
    ]
    tots_ref[0] = tot_ref[...]

    quarter = rows // NX
    half = quarter // 2
    relays = {}
    x_copies = {}
    x_dev = [(v, (x + 1) % NX * NZ + zh), (v, (x + 3) % NX * NZ + zh)]

    def rows_of(j, lo=0, size=quarter):
        return pl.ds(pl.multiple_of((x + j) % NX * quarter + lo, half), size)

    def along_x(n):
        for d in range(2):
            relays[n, d].wait_recv()
            part = rows_of(1 + 2 * d, d * half, half)
            c_ref[n, part] = c_ref[n, part] + relay_ref[d, n]
            x_copies[n, d] = go(remote(
                c_ref.at[n, rows_of(1 + 2 * d)], xr_ref.at[d, n],
                x_send.at[n, d], x_recv.at[n, d], x_dev[d],
            ))

    for n in range(NB):
        loads[n].wait()
        c_ref[n] = lax.dot_general(
            u_ref[...], b_ref[n], (((1,), (1,)), ((), ())), preferred_element_type=F32
        )
        for d in range(2):
            relays[n, d] = go(remote(
                c_ref.at[n, rows_of(2, d * half, half)], relay_ref.at[d, n],
                r_send.at[n, d], r_recv.at[n, d], x_dev[d],
            ))
        if n:
            along_x(n - 1)
    along_x(NB - 1)

    each = quarter // NZ
    per = NB // GROUPS
    z_copies = {}
    for h in range(GROUPS):
        for n in range(h * per, (h + 1) * per):
            for d in range(2):
                x_copies[n, d].wait_recv()
            d_ref[n] = (c_ref[n, rows_of(0)] + xr_ref[0, n]) + xr_ref[1, n]
        part = pl.ds(h * per, per)
        for j in (2, 1, 3):
            zz = (zh + j) % NZ
            z_copies[h, j] = go(remote(
                d_ref.at[part, pl.ds(zz * each, each)], zr_ref.at[j, part],
                z_send.at[h, j], z_recv.at[h, j], (v, x * NZ + zz),
            ))

    for c in tot_copies:
        c.wait_recv()
    total = jnp.zeros((8, rows), F32)
    for q in range(n_state):
        total = total + tots_ref[(s + n_state - q) % n_state]
    tcol_ref[...] = jnp.transpose(jnp.broadcast_to(total[0:1], (rows, rows)))

    def norm(i, carry):
        cols = pl.ds(pl.multiple_of(i * rows, rows), rows)
        new_ref[:, cols] = ((scale * unnorm_ref[:, cols]) / tcol_ref[...]).astype(BF16)
        return carry

    lax.fori_loop(0, unnorm_ref.shape[1] // rows, norm, 0)

    best = None
    for h in range(GROUPS):
        for j in range(1, NZ):
            z_copies[h, j].wait_recv()
        for n in range(h * per, (h + 1) * per):
            mine = d_ref[n, pl.ds(pl.multiple_of(zh * each, each), each)]
            full = (mine + zr_ref[1, n]) + (zr_ref[2, n] + zr_ref[3, n])
            best = full if best is None else jnp.maximum(best, full)
    top = jnp.max(best, axis=1, keepdims=True)
    mine = tcol_ref[pl.ds(pl.multiple_of(s * each, each), each)]
    val_ref[...] = jnp.broadcast_to(top, mine.shape) / mine
    for c in sends:
        c.wait_send()


def scores(unnorm, u, tot, alphas_all, scale):
    rows, cols = u.shape
    n_alpha = alphas_all.shape[0]
    wide = n_alpha // NB
    quarter = rows // NX
    n_state = NX * NZ
    dma = pltpu.SemaphoreType.DMA
    vmem = pl.BlockSpec(memory_space=pltpu.VMEM)
    return pl.pallas_call(
        functools.partial(score_kernel, scale),
        out_shape=(
            jax.ShapeDtypeStruct((rows, cols), BF16),
            jax.ShapeDtypeStruct((rows // n_state, rows), F32),
        ),
        in_specs=[vmem, vmem, vmem, pl.BlockSpec(memory_space=pl.ANY)],
        out_specs=(vmem, vmem),
        scratch_shapes=[
            pltpu.VMEM((NB, wide, cols), BF16),
            pltpu.VMEM((NB, rows, wide), F32),
            pltpu.VMEM((2, NB, quarter // 2, wide), F32),
            pltpu.VMEM((2, NB, quarter, wide), F32),
            pltpu.VMEM((NB, quarter, wide), F32),
            pltpu.VMEM((NZ, NB, quarter // NZ, wide), F32),
            pltpu.VMEM((n_state, 8, rows), F32),
            pltpu.VMEM((rows, rows), F32),
            dma((NB,)), dma((n_state,)), dma((n_state,)),
            dma((NB, 2)), dma((NB, 2)), dma((NB, 2)), dma((NB, 2)), dma((GROUPS, NZ)), dma((GROUPS, NZ)),
        ],
        compiler_params=pltpu.CompilerParams(
            collective_id=1, has_side_effects=True, vmem_limit_bytes=BIG
        ),
    )(unnorm, u, tot, alphas_all)


def per_device(
    beliefs, tiles, tile_src, tile_dst, tile_action, obs_prob, action_index, obs_index, alphas
):
    n_vec = lax.axis_size("vec")
    n_state = lax.axis_size("state")
    rows, cols = beliefs.shape
    act_row = action_index[None, :]
    src, alphas_all = exchange(tile_src[None, :], tile_action[None, :], act_row, beliefs, alphas, n_vec)
    unnorm, u, tot = tile_products(
        tile_action, tile_dst, act_row, obs_index[None, :], src, tiles, obs_prob.reshape(ACT * OBS, cols)
    )
    new_belief, value = scores(
        unnorm, u, tot, alphas_all.reshape(n_vec * rows, cols), float(cols * n_state)
    )
    return new_belief, value[:, 0]


def solution(mesh):
    placed = (
        P("vec", "state"),
        P("state", None, None),
        P("state"),
        P("state"),
        P("state"),
        P(None, None, "state"),
        P("vec"),
        P("vec"),
        P("vec", "state"),
    )
    return jax.shard_map(
        per_device,
        mesh=mesh,
        in_specs=placed,
        out_specs=(P("vec", "state"), P(("vec", "state"))),
        check_vma=False,
    )
```

time: 116 us -> 121 us (1.043)
  Pallas kernels: 101 us -> 114 us
  local copies, waits for them, and re-layouts: 9.63 us -> 3.18 us
  other arithmetic: 3.66 us -> 0 us
    unnamed x11 -> x1, local copies, waits for them, and re-layouts: 8.13 us -> 1.88 us
    pallas_call x1, Pallas kernels: 3.98 us -> 9.9 us  [tile_products(): pl.pallas_call(tiles_kernel, out_shape=(jax.ShapeDtypeStruct((rows, cols)...]
    pallas_call x1, Pallas kernels: 25.1 us -> 29.8 us  [scores(): pl.pallas_call(functools.partial(score_kernel, scale), out_shape=(jax.Sha...]
    pallas_call x1, Pallas kernels: 71.5 us -> 74.8 us  [exchange(): pl.pallas_call(exchange_kernel, out_shape=(jax.ShapeDtypeStruct((KS, rows...]
    reduce_sum x2 -> x0, other arithmetic: 1.65 us -> none  [the longest x1 0.91 us: per_device(): rank = jnp.sum(earlier.astype(jnp.int32), axis=1)]
where the time goes in v2:
time: 121 us; the launch traced here: 118 us
  Pallas kernels  114 us (94%)
  local copies, waits for them, and re-layouts  3.18 us (3%)
    pallas_call x1, Pallas kernels, exchange(): pl.pallas_call(exchange_kernel, out_shape=(jax.ShapeDtypeStruct((KS, rows...  74.8 us
    pallas_call x1, Pallas kernels, scores(): pl.pallas_call(functools.partial(score_kernel, scale), out_shape=(jax.Sha...  29.8 us
    pallas_call x1, Pallas kernels, tile_products(): pl.pallas_call(tiles_kernel, out_shape=(jax.ShapeDtypeStruct((rows, cols)...  9.9 us

profile of v2, /device:TPU:1, one launch (start us, length us, event | category | flops | bytes accessed | tf_op | source)
XLA Modules:
  0.0 118.3 jit_solution(922925577013883692)
XLA Ops:
  0.6 74.8 %shard_map.104 = (bf16[8,128,256]{2,1,0:T(8,128)(2,1)}, bf16[16,128,2048]{2,1,0:T(8,128)(2,1)}) custom-call(s32[1,64]{1,0:T(1,128)} %bitcast.11, s32[1,64]{1,0:T(1,128)} %bitcast.8, s32[1,128]{1,0:T(1,128)} %bitcast.9, bf16[128,2048]{1,0:T(8,128)(2,1)} %bel_ref.1, bf16[128,2048]{1,0:T(8,128)(2,1)} %alp_ref.1), custom_call_target="tpu_custom_call" | custom-call | tf_op jit(solution)/shard_map/pallas_call | solution.py:260
  75.4 9.9 %shard_map.105 = (f32[128,2048]{1,0:T(8,128)}, bf16[128,2048]{1,0:T(8,128)(2,1)}, f32[8,128]{1,0:T(8,128)}) custom-call(s32[64]{0:T(128)} %sact_ref.1, s32[64]{0:T(128)} %dst_ref.1, s32[1,128]{1,0:T(1,128)} %bitcast.10, s32[1,128]{1,0:T(1,128)} %bitcast.12, bf16[8,128,256]{2,1,0:T(8,128)(2,1)} %get-tuple-element.9.src_ref, bf16[64,256,256]{2,1,0:T(8,128)(2,1)} %tiles_ref.1, ...), custom_call_target="tpu_custom_call" | custom-call | tf_op jit(solution)/shard_map/pallas_call | solution.py:339
  85.3 29.8 %shard_map.106 = (bf16[128,2048]{1,0:T(8,128)(2,1)}, f32[8,128]{1,0:T(8,128)}) custom-call(f32[128,2048]{1,0:T(8,128)} %get-tuple-element.10.unnorm_ref, bf16[128,2048]{1,0:T(8,128)(2,1)} %get-tuple-element.11.u_ref, f32[8,128]{1,0:T(8,128)} %get-tuple-element.12.tot_ref, bf16[2048,2048]{1,0:T(8,128)(2,1)} %bitcast.6), custom_call_target="tpu_custom_call" | custom-call | tf_op jit(solution)/shard_map/pallas_call | solution.py:486
  115.1 1.3 %slice_reduce_fusion = f32[8]{0:T(128)} fusion(f32[8,128]{1,0:T(8,128)} %get-tuple-element.15), kind=kLoop, calls=%fused_computation | loop fusion | bytes 64 | tf_op jit(solution)/shard_map/slice | solution.py:526
  116.4 1.9 %copy.12 = bf16[128,2048]{1,0:T(8,128)(2,1)} copy(bf16[128,2048]{1,0:T(8,128)(2,1)} %get-tuple-element.18) | data formatting | bytes 1048576

commit v3 on v0

v3 whole, which is shorter than its diff:
```python
import functools

import jax
import jax.numpy as jnp
from jax import lax
from jax.experimental import pallas as pl
from jax.experimental.pallas import tpu as pltpu
from jax.sharding import PartitionSpec as P

TILE = 256
ACT = 8
OBS = 32
KS = 8
NX = 4
NZ = 4
PIECE_ROWS = (32, 32, 32, 16, 16)
NB = 8
GROUPS = 4
BIG = 62 << 20
MESH = pl.DeviceIdType.MESH
F32 = jnp.float32
BF16 = jnp.bfloat16


def remote(src, dst, send, recv, dev):
    return pltpu.make_async_remote_copy(
        src_ref=src, dst_ref=dst, send_sem=send, recv_sem=recv, device_id=dev, device_id_type=MESH
    )


def greet(devs):
    for dev in devs:
        pl.semaphore_signal(
            pltpu.get_barrier_semaphore(), inc=1, device_id=dev, device_id_type=MESH
        )


def all_here(devs):
    pl.semaphore_wait(pltpu.get_barrier_semaphore(), len(devs))


def expand_kernel(
    scale, tsrc_ref, tact_ref, tdst_ref, act_ref, seen_ref, bel_ref, alp_ref, tiles_hbm, obs_hbm,
    new_ref, val_ref, *scratch,
):
    scratch = list(scratch)
    n_p = len(PIECE_ROWS)
    g_refs, scratch = scratch[:n_p], scratch[n_p:]
    m_refs, scratch = scratch[:n_p], scratch[n_p:]
    (
        pick_ref, land_ref, r_ref, full_ref, tabs_ref, slot_ref, smem_ref, slot_smem,
        tiles_ref, obs_ref, seg_ref, unnorm_ref, u_ref, b_ref, c_ref, xr_ref, d_ref, zr_ref,
        tot_ref, totx_ref, totz_ref, tcol_ref,
        bel_sem, loc_sem, tab_send, tab_recv, z_send, z_recv, f_send, f_recv, x_send, x_recv,
        b_send, b_recv, cx_send, cx_recv, cz_send, cz_recv, t_send, t_recv,
    ) = scratch
    v = lax.axis_index("vec")
    s = lax.axis_index("state")
    x, zh = s // NZ, s % NZ
    y, zl, core = v // 4, (v // 2) % 2, v % 2
    rows, cols = bel_ref.shape
    kh = KS // 2
    starts = [sum(PIECE_ROWS[:p]) for p in range(n_p)]

    def at_vec(yy, ll, cc):
        return (yy * 4 + ll * 2 + cc, s)

    x_dev = [(v, (x + j) % NX * NZ + zh) for j in range(1, NX)]
    z_all = [(v, x * NZ + (zh + j) % NZ) for j in range(1, NZ)]
    z_dev = [z_all[0], z_all[2]]
    y_dev = [at_vec((y + 1) % 4, zl, core), at_vec((y + 3) % 4, zl, core)]
    pair_dev = at_vec(y, 1 - zl, core)
    sib_dev = at_vec(y, zl, 1 - core)
    near = x_dev + z_all + y_dev + [pair_dev, sib_dev]
    greet(near)

    def block(yy, ll, lo=0, n=rows):
        return b_ref.at[yy * 2 + ll, pl.ds(pl.multiple_of(core * rows + lo, 16), n)]

    own_bel = {}
    for p in range(n_p):
        for t in range(KS):
            own_bel[p, t] = pltpu.make_async_copy(
                bel_ref.at[pl.ds(starts[p], PIECE_ROWS[p]), pl.ds(t * TILE, TILE)],
                g_refs[p].at[zh * KS + t], bel_sem.at[p, t],
            )
            own_bel[p, t].start()
    mine = block(y, zl)
    own_alp = pltpu.make_async_copy(alp_ref, mine, loc_sem.at[0])
    own_alp.start()
    own_obs = pltpu.make_async_copy(obs_hbm, obs_ref, loc_sem.at[1])
    own_tiles = pltpu.make_async_copy(tiles_hbm, tiles_ref, loc_sem.at[2])

    nt = tact_ref.shape[1]
    act_l = jnp.broadcast_to(tact_ref[...].astype(F32), (nt, nt))
    dst_l = jnp.broadcast_to((tdst_ref[...] & (cols // TILE - 1)).astype(F32), (nt, nt))
    src_s = jnp.transpose(jnp.broadcast_to(tsrc_ref[...].astype(F32), (nt, nt)))
    act_s, dst_s = jnp.transpose(act_l), jnp.transpose(dst_l)
    sub = lax.broadcasted_iota(jnp.int32, (nt, nt), 0)
    lan = lax.broadcasted_iota(jnp.int32, (nt, nt), 1)
    one = jnp.ones((nt, nt), F32)
    nil = jnp.zeros((nt, nt), F32)
    rank = jnp.sum(jnp.where((act_l == act_s) & (lan < sub), one, nil), axis=1, keepdims=True)
    lane = lax.broadcasted_iota(jnp.int32, (nt, 128), 1).astype(F32)
    by_rank = jnp.where(rank == lane, 1.0, 0.0).astype(BF16)
    by_act = jnp.where(act_s[:, :1] == lane, src_s[:, :1], 0.0).astype(BF16)
    table = lax.dot_general(by_rank, by_act, (((0,), (0,)), ((), ())), preferred_element_type=F32)
    tabs_ref[0] = table[:KS].astype(jnp.int32)
    rank_row = jnp.sum(jnp.where((act_l == act_s) & (sub < lan), one, nil), axis=0, keepdims=True)
    same_row = jnp.sum(jnp.where((dst_l == dst_s) & (sub < lan), one, nil), axis=0, keepdims=True)
    place = jnp.where((dst_l < dst_s) | ((dst_l == dst_s) & (lan < sub)), one, nil)
    place = jnp.sum(place, axis=1, keepdims=True)
    by_place = jnp.where(place == lane, 1.0, 0.0).astype(BF16)
    row8 = lax.broadcasted_iota(jnp.int32, (8, nt), 0)
    facts = jnp.where(row8 == 0, act_l[:8], jnp.where(row8 == 1, jnp.broadcast_to(rank_row, (8, nt)), 0.0))
    facts = jnp.where(row8 == 2, lan[:8].astype(F32), facts)
    facts = jnp.where(row8 == 3, jnp.broadcast_to(jnp.minimum(same_row, 1.0), (8, nt)), facts)
    slot_tab = jnp.dot(facts.astype(BF16), by_place, preferred_element_type=F32)
    upto = jnp.sum(jnp.where(dst_s[:, :1] <= lane, 1.0, 0.0), axis=0, keepdims=True)
    here = jnp.sum(jnp.where(dst_s[:, :1] == lane, 1.0, 0.0), axis=0, keepdims=True)
    last = jnp.broadcast_to(jnp.maximum(upto - 1.0, 0.0), (8, 128))
    some = jnp.broadcast_to(jnp.minimum(here, 1.0), (8, 128))
    row8 = lax.broadcasted_iota(jnp.int32, (8, 128), 0)
    slot_tab = jnp.where(row8 == 4, last, jnp.where(row8 == 5, some, slot_tab))
    slot_ref[...] = slot_tab.astype(jnp.int32)

    act_col = jnp.transpose(jnp.broadcast_to(act_ref[...].astype(F32), (rows, rows)))
    for p in range(n_p):
        m_refs[p][...] = jnp.zeros_like(m_refs[p])
    for a in range(ACT):
        hit = jnp.where(act_col == float(a), 1.0, 0.0).astype(BF16)
        for c in range(TILE // rows):
            part = slice(c * rows, (c + 1) * rows)
            full_ref[a, :, part] = hit
            for p in range(n_p):
                m_refs[p][a * NX, :, part] = hit[starts[p] : starts[p] + PIECE_ROWS[p]]

    for c in own_bel.values():
        c.wait()
    all_here(near)

    sends = []

    def go(c):
        c.start()
        sends.append(c)
        return c

    def own_send(p, d):
        part = g_refs[p].at[pl.ds(zh * KS, KS)]
        return remote(part, part, z_send.at[d, p], z_recv.at[d, p], z_dev[d])

    def forward(p, d):
        origin = (zh + 3) % NZ if d == 0 else (zh + 1) % NZ
        part = g_refs[p].at[pl.ds(origin * KS + d * kh, kh)]
        return remote(part, part, f_send.at[d, p], f_recv.at[d, p], z_dev[d])

    own = {}
    for p in range(2):
        for d in range(2):
            own[p, d] = go(own_send(p, d))

    tab_copies = [
        go(remote(tabs_ref.at[0], tabs_ref.at[j], tab_send.at[j], tab_recv.at[j], x_dev[j - 1]))
        for j in range(1, NX)
    ]

    n_b = [0]

    def b_copy(part, dev):
        i = n_b[0]
        n_b[0] += 1
        return go(remote(part, part, b_send.at[i], b_recv.at[i], dev))

    own_alp.wait()
    own_tiles.start()
    own_obs.start()
    b_up = b_copy(mine, y_dev[0])
    b_down = b_copy(mine, y_dev[1])
    b_sib = [b_copy(mine, sib_dev)]
    p_sib = [[], []]
    half = rows // 2

    def ring_forward(ll, lo, n, up, down, sib):
        up.wait_recv()
        one = b_copy(block((y + 3) % 4, ll, lo, n // 2), y_dev[0])
        down.wait_recv()
        two = b_copy(block((y + 1) % 4, ll, lo + n // 2, n // 2), y_dev[1])
        for yy in ((y + 3) % 4, (y + 1) % 4):
            sib.append(b_copy(block(yy, ll, lo, n), sib_dev))
        return one, two

    def ring_end(ll, lo, n, stage, sib):
        stage[0].wait_recv()
        stage[1].wait_recv()
        sib.append(b_copy(block((y + 2) % 4, ll, lo, n), sib_dev))

    for c in tab_copies:
        c.wait_recv()
    to_smem = pltpu.make_async_copy(tabs_ref, smem_ref, loc_sem.at[3])
    to_smem.start()
    slots_to_smem = pltpu.make_async_copy(slot_ref, slot_smem, loc_sem.at[4])
    slots_to_smem.start()
    to_smem.wait()
    slots_to_smem.wait()

    def pick(j, p, into):
        part = pl.ds(starts[p], PIECE_ROWS[p])

        def one(k, carry):
            acc = None
            for a in range(ACT):
                src = smem_ref[(NX - j) % NX, k, a]
                tile = g_refs[p][src & (NZ * KS - 1)]
                away = ((src >> 5) + NX - x) & (NX - 1)
                m = m_refs[p][a * NX + away]
                acc = tile * m if acc is None else acc + tile * m
            into[k, part] = acc
            return carry

        lax.fori_loop(0, KS, one, 0)

    fwd = {}
    x_copies = []

    def along_x(p):
        part = pl.ds(starts[p], PIECE_ROWS[p])
        fwd[p, 0].wait_recv()
        fwd[p, 1].wait_recv()
        for j in (2, 1, 3):
            pick(j, p, pick_ref.at[j - 1])
            x_copies.append(go(remote(
                pick_ref.at[j - 1, :, part], land_ref.at[j, :, part],
                x_send.at[j, p], x_recv.at[j, p], x_dev[j - 1],
            )))
        pick(0, p, land_ref.at[0])

    partner = 1 - zl
    for p in range(n_p):
        for d in range(2):
            own[p, d].wait_recv()
            fwd[p, d] = go(forward(p, d))
        if p + 2 < n_p:
            for d in range(2):
                own[p + 2, d] = go(own_send(p + 2, d))
        if p == n_p - 1:
            pair = [b_copy(block(y, zl, c * half, half), pair_dev) for c in range(2)]
        if p == 1:
            stage = ring_forward(zl, 0, rows, b_up, b_down, b_sib)
        if p == 2:
            ring_end(zl, 0, rows, stage, b_sib)
        if p:
            along_x(p - 1)
    along_x(n_p - 1)

    def partner_out(c):
        pair[c].wait_recv()
        part = block(y, partner, c * half, half)
        out = b_copy(part, y_dev[0]), b_copy(part, y_dev[1])
        p_sib[c].append(b_copy(part, sib_dev))
        return out

    for c in x_copies:
        c.wait_recv()

    def merge(k, carry):
        r_ref[k] = (land_ref[0, k] + land_ref[1, k]) + (land_ref[2, k] + land_ref[3, k])
        return carry

    lax.fori_loop(0, KS, merge, 0)
    round0 = partner_out(0)

    own_tiles.wait()
    own_obs.wait()
    seg_ref[0] = jnp.zeros_like(seg_ref[0])

    def eight(o, carry):
        for e in range(8):
            i = o * 8 + e
            left = r_ref[slot_smem[1, i] & (KS - 1)] * full_ref[slot_smem[0, i] & (ACT - 1)]
            part = jnp.dot(left, tiles_ref[slot_smem[2, i] & (nt - 1)], preferred_element_type=F32)
            seg_ref[i + 1] = seg_ref[i] * slot_smem[3, i].astype(F32) + part
        return carry

    lax.fori_loop(0, nt // 8, eight, 0)

    code = act_ref[...] * OBS + seen_ref[...]
    codes = lax.broadcasted_iota(jnp.int32, (ACT * OBS, rows), 0)
    hot = jnp.where(codes == code, 1.0, 0.0).astype(BF16)
    total = jnp.zeros((rows, 1), F32)
    for d in range(cols // TILE):
        part = pl.ds(d * TILE, TILE)
        seen = lax.dot_general(
            hot, obs_ref[:, part], (((0,), (0,)), ((), ())), preferred_element_type=F32
        )
        reached = seg_ref[(slot_smem[4, d] & (nt - 1)) + 1] * slot_smem[5, d].astype(F32)
        un = reached * seen
        unnorm_ref[:, part] = un
        u_ref[:, part] = un.astype(BF16)
        total = total + jnp.sum(un, axis=1, keepdims=True)
    tot_ref[...] = jnp.transpose(jnp.broadcast_to(total, (rows, rows)))[:8]

    tot_x = [
        go(remote(tot_ref, totx_ref.at[j], t_send.at[0, j], t_recv.at[0, j], x_dev[j - 1]))
        for j in range(1, NX)
    ]

    quarter = rows // NX
    cx = {}

    def score(n, yy, ll):
        c_ref[n] = lax.dot_general(
            u_ref[...], b_ref[yy * 2 + ll], (((1,), (1,)), ((), ())), preferred_element_type=F32
        )
        for j in (2, 1, 3):
            xx = (x + j) % NX
            cx[n, j] = go(remote(
                c_ref.at[n, pl.ds(pl.multiple_of(xx * quarter, quarter), quarter)], xr_ref.at[j, n],
                cx_send.at[n, j], cx_recv.at[n, j], x_dev[j - 1],
            ))

    each = quarter // NZ
    per = NB // GROUPS
    cz = {}

    def along_z(h):
        for n in range(h * per, (h + 1) * per):
            for j in range(1, NX):
                cx[n, j].wait_recv()
            own_part = c_ref[n, pl.ds(pl.multiple_of(x * quarter, quarter), quarter)]
            d_ref[n] = (own_part + xr_ref[1, n]) + (xr_ref[2, n] + xr_ref[3, n])
        part = pl.ds(h * per, per)
        for j in (2, 1, 3):
            zz = (zh + j) % NZ
            cz[h, j] = go(remote(
                d_ref.at[part, pl.ds(pl.multiple_of(zz * each, each), each)], zr_ref.at[j, part],
                cz_send.at[h, j], cz_recv.at[h, j], z_all[j - 1],
            ))

    for c in b_sib:
        c.wait_recv()
    for i in range(4):
        score(i, (y + i) % 4, zl)
    round1 = partner_out(1)
    stage0 = ring_forward(partner, 0, half, *round0, p_sib[0])
    for c in tot_x:
        c.wait_recv()
    totx_ref[0] = (tot_ref[...] + totx_ref[1]) + (totx_ref[2] + totx_ref[3])
    tot_z = [
        go(remote(totx_ref.at[0], totz_ref.at[j], t_send.at[1, j], t_recv.at[1, j], z_all[j - 1]))
        for j in range(1, NZ)
    ]
    along_z(0)
    stage1 = ring_forward(partner, half, half, *round1, p_sib[1])
    along_z(1)
    ring_end(partner, 0, half, stage0, p_sib[0])
    for c in range(2):
        p_sib[c][0].wait_recv()
    score(4, y, partner)
    for c in range(2):
        p_sib[c][1].wait_recv()
        p_sib[c][2].wait_recv()
    score(5, (y + 1) % 4, partner)
    score(6, (y + 3) % 4, partner)
    ring_end(partner, half, half, stage1, p_sib[1])
    for c in range(2):
        p_sib[c][3].wait_recv()
    score(7, (y + 2) % 4, partner)

    for c in tot_z:
        c.wait_recv()
    all_tot = (totx_ref[0] + totz_ref[1]) + (totz_ref[2] + totz_ref[3])
    tcol_ref[...] = jnp.transpose(jnp.broadcast_to(all_tot[0:1], (rows, rows)))

    def norm(i, carry):
        part = pl.ds(pl.multiple_of(i * rows, rows), rows)
        new_ref[:, part] = ((scale * unnorm_ref[:, part]) / tcol_ref[...]).astype(BF16)
        return carry

    lax.fori_loop(0, cols // rows, norm, 0)
    along_z(2)
    along_z(3)

    best = None
    for h in range(GROUPS):
        for j in range(1, NZ):
            cz[h, j].wait_recv()
        for n in range(h * per, (h + 1) * per):
            own_part = d_ref[n, pl.ds(pl.multiple_of(zh * each, each), each)]
            full = (own_part + zr_ref[1, n]) + (zr_ref[2, n] + zr_ref[3, n])
            best = full if best is None else jnp.maximum(best, full)
    top = jnp.max(best, axis=1, keepdims=True)
    div = tcol_ref[pl.ds(pl.multiple_of(s * each, each), each)]
    val_ref[...] = jnp.broadcast_to(top, div.shape) / div
    for c in sends:
        c.wait_send()


def per_device(
    beliefs, tiles, tile_src, tile_dst, tile_action, obs_prob, action_index, obs_index, alphas
):
    n_vec = lax.axis_size("vec")
    n_state = lax.axis_size("state")
    rows, cols = beliefs.shape
    nt = tile_src.shape[0]
    wide = n_vec * alphas.shape[0] // NB
    quarter = rows // NX
    n_p = len(PIECE_ROWS)
    dma = pltpu.SemaphoreType.DMA
    vmem = pl.BlockSpec(memory_space=pltpu.VMEM)
    hbm = pl.BlockSpec(memory_space=pl.ANY)
    new_belief, value = pl.pallas_call(
        functools.partial(expand_kernel, float(cols * n_state)),
        out_shape=(
            jax.ShapeDtypeStruct((rows, cols), BF16),
            jax.ShapeDtypeStruct((rows // n_state, rows), F32),
        ),
        in_specs=[vmem, vmem, vmem, vmem, vmem, hbm, hbm, hbm, hbm],
        out_specs=(vmem, vmem),
        scratch_shapes=[
            *[pltpu.VMEM((NZ * KS, r, TILE), BF16) for r in PIECE_ROWS],
            *[pltpu.VMEM((ACT * NX, r, TILE), BF16) for r in PIECE_ROWS],
            pltpu.VMEM((NX - 1, KS, rows, TILE), BF16),
            pltpu.VMEM((NX, KS, rows, TILE), BF16),
            pltpu.VMEM((KS, rows, TILE), BF16),
            pltpu.VMEM((ACT, rows, TILE), BF16),
            pltpu.VMEM((NX, 8, 128), jnp.int32),
            pltpu.VMEM((8, 128), jnp.int32),
            pltpu.SMEM((NX, 8, 128), jnp.int32),
            pltpu.SMEM((8, 128), jnp.int32),
            pltpu.VMEM(tiles.shape, BF16),
            pltpu.VMEM((ACT * OBS, cols), BF16),
            pltpu.VMEM((nt + 1, rows, TILE), F32),
            pltpu.VMEM((rows, cols), F32),
            pltpu.VMEM((rows, cols), BF16),
            pltpu.VMEM((NB, wide, cols), BF16),
            pltpu.VMEM((NB, rows, wide), F32),
            pltpu.VMEM((NX, NB, quarter, wide), F32),
            pltpu.VMEM((NB, quarter, wide), F32),
            pltpu.VMEM((NZ, NB, quarter // NZ, wide), F32),
            pltpu.VMEM((8, rows), F32),
            pltpu.VMEM((NX, 8, rows), F32),
            pltpu.VMEM((NZ, 8, rows), F32),
            pltpu.VMEM((rows, rows), F32),
            dma((n_p, KS)), dma((5,)), dma((NX,)), dma((NX,)),
            dma((2, n_p)), dma((2, n_p)), dma((2, n_p)), dma((2, n_p)),
            dma((NX, n_p)), dma((NX, n_p)), dma((32,)), dma((32,)),
            dma((NB, NX)), dma((NB, NX)), dma((GROUPS, NZ)), dma((GROUPS, NZ)),
            dma((2, NX)), dma((2, NX)),
        ],
        compiler_params=pltpu.CompilerParams(
            collective_id=0, has_side_effects=True, vmem_limit_bytes=BIG
        ),
    )(
        tile_src[None, :], tile_action[None, :], tile_dst[None, :], action_index[None, :],
        obs_index[None, :], beliefs, alphas, tiles, obs_prob.reshape(ACT * OBS, cols),
    )
    return new_belief, value[:, 0]


def solution(mesh):
    placed = (
        P("vec", "state"),
        P("state", None, None),
        P("state"),
        P("state"),
        P("state"),
        P(None, None, "state"),
        P("vec"),
        P("vec"),
        P("vec", "state"),
    )
    return jax.shard_map(
        per_device,
        mesh=mesh,
        in_specs=placed,
        out_specs=(P("vec", "state"), P(("vec", "state"))),
        check_vma=False,
    )
```

time: 389 us -> 94.7 us (0.24)
  the two profiles are of different devices: /device:TPU:1 before, /device:TPU:32 now
where the time goes in v3:
time: 94.7 us; the launch traced here: 94.5 us
  Pallas kernels  90.6 us (96%)
  local copies, waits for them, and re-layouts  3.19 us (3%)
    pallas_call x1, Pallas kernels, per_device(): pl.pallas_call(functools.partial(expand_kernel, float(cols * n_state)), o...  90.6 us

profile of v3, /device:TPU:32, one launch (start us, length us, event | category | flops | bytes accessed | tf_op | source)
XLA Modules:
  0.0 94.5 jit_solution(2663422307366049292)
XLA Ops:
  0.6 90.6 %shard_map.104 = (bf16[128,2048]{1,0:T(8,128)(2,1)}, f32[8,128]{1,0:T(8,128)}) custom-call(s32[1,64]{1,0:T(1,128)} %bitcast.7, s32[1,64]{1,0:T(1,128)} %bitcast.8, s32[1,64]{1,0:T(1,128)} %bitcast.9, s32[1,128]{1,0:T(1,128)} %bitcast.10, s32[1,128]{1,0:T(1,128)} %bitcast.11, bf16[128,2048]{1,0:T(8,128)(2,1)} %bel_ref.1, bf16[128,2048]{1,0:T(8,128)(2,1)} %alp_ref.1, ...), custom_call_target="tpu_custom_call" | custom-call | tf_op jit(solution)/shard_map/pallas_call | solution.py:412
  91.3 1.3 %slice_reduce_fusion = f32[8]{0:T(128)} fusion(f32[8,128]{1,0:T(8,128)} %get-tuple-element.5), kind=kLoop, calls=%fused_computation | loop fusion | bytes 64 | tf_op jit(solution)/shard_map/slice | solution.py:458
  92.6 1.9 %copy.12 = bf16[128,2048]{1,0:T(8,128)(2,1)} copy(bf16[128,2048]{1,0:T(8,128)(2,1)} %get-tuple-element.8) | data formatting | bytes 1048576
